TPU v7x, 128 devices: a whole 4x4x4 slice. The times are simulated.
128 devices in a mesh: req: 32 (over x, z, core), tp: 4 (over y).
Axes of the slice: x: 4, y: 4, z: 4, core: 2. Of those that a mesh axis runs over, the one named last changes fastest.
Arguments:
- tokens: bfloat16 [1024, 2048], P('req'), may hold values from -6 to 6
- deal_order: int32 [1024], replicated, may hold values from 0 to 1023, as said below
- page_table: int32 [1024, 6], P('req'), may hold values from 0 to 1343, as said below
- lengths: int32 [1024], P('req'), may hold values from 1 to 768, as said below
- qkv_weight: bfloat16 [2048, 3, 2048], P(None, None, 'tp'), may hold values from -0.125 to 0.125
- out_weight: bfloat16 [2048, 2048], P('tp'), may hold values from -0.125 to 0.125
- up_weight: bfloat16 [2048, 4096], P(None, 'tp'), may hold values from -0.125 to 0.125
- down_weight: bfloat16 [4096, 2048], P('tp'), may hold values from -0.09375 to 0.09375
- key_cache: bfloat16 [2, 1344, 128, 2048], P(None, 'req', None, 'tp')
- value_cache: bfloat16 [2, 1344, 128, 2048], P(None, 'req', None, 'tp'), may hold values from -6 to 6
- attn_norm: float32 [2, 2048], replicated
- mlp_norm: float32 [2, 2048], replicated
Outputs:
- output: bfloat16 [1024, 2048], P('req')
Inputs may be any that keep to these rules, and one draw needn't show every extreme that they name: `deal_order`: A permutation: every request is placed in exactly one slot. Of the 32 requests in the slots s // 32 = d of one block d, at most 2 come from one source block of rows r // 32 = j, and some pair of blocks has exactly 2. `page_table`: row s holds the pages of the request in dealt slot s: its first ceil(lengths[s] / 128) entries are pages of the block s // 32 * 42 to s // 32 * 42 + 41, no page serves two slots, and the remaining entries repeat the row's first page. `lengths`: A request fills at most 6 pages; the slots s // 32 = d of one block d fill at most 42 pages together, and some block fills exactly that many.
All inputs are finite; a program needn't handle non-finite values.
Results may differ from a plain program's by a relative error of at most 0.034.
Values may be sent and summed in bfloat16 or wider, within the bound.
No kernel may reach another device: no remote copies, remote signals or barrier semaphores. Data moves between devices by JAX's collectives and lax.ppermute only.
A program may use at most 448 MiB of HBM per device.

v0:
```python
import math
import jax
import jax.numpy as jnp
from jax import lax
from jax.sharding import PartitionSpec as P

HD = 128
epsilon = 1e-06


def layer_norm(row_total, gain_bias):
    row_mean = jnp.mean(row_total, axis=-1, keepdims=True)
    centered = row_total - row_mean
    row_var = jnp.mean(centered * centered, axis=-1, keepdims=True)
    return (centered * lax.rsqrt(row_var + epsilon) * gain_bias[0] + gain_bias[1]).astype(
        jnp.bfloat16
    )


def post_norm(partial_term, residual, gain_bias):
    row_total = lax.psum(partial_term.astype(jnp.bfloat16), "tp").astype(
        jnp.float32
    ) + residual.astype(jnp.float32)
    return layer_norm(row_total, gain_bias)


def head_masks(feat_share, head_dim):
    head_count = feat_share // head_dim
    owner = jnp.arange(feat_share, dtype=jnp.int32) // head_dim
    return owner[None, :] == jnp.arange(head_count, dtype=jnp.int32)[:, None]


def spread_query(query_flat, mask):
    return jnp.where(mask[None, :, :], query_flat[:, None, :], jnp.zeros((), query_flat.dtype))


def own_scores(query_flat, key_new, mask, score_scale):
    product = query_flat.astype(jnp.float32) * key_new.astype(jnp.float32)
    return jnp.sum(jnp.where(mask[None, :, :], product[:, None, :], 0.0), axis=-1) * score_scale


def finish_mix(scores, own_score, value_new, mask, mix_fn):
    row_max = jnp.maximum(jnp.max(scores, axis=-1), own_score)
    exp_cache = jnp.exp(scores - row_max[..., None])
    exp_own = jnp.exp(own_score - row_max)
    row_total = jnp.sum(exp_cache, axis=-1) + exp_own
    cache_weights = (exp_cache / row_total[..., None]).astype(jnp.bfloat16)
    own_weight = (exp_own / row_total).astype(jnp.bfloat16).astype(jnp.float32)
    mixed_wide = mix_fn(cache_weights)
    mixed_cache = jnp.sum(jnp.where(mask[None, :, :], mixed_wide, 0.0), axis=1)
    own_spread = jnp.sum(jnp.where(mask[None, :, :], own_weight[:, :, None], 0.0), axis=1)
    return mixed_cache + own_spread * value_new.astype(jnp.float32)


def attend_pool(
    query_flat, key_new, value_new, key_pool, value_pool, local_table, lengths, score_scale, mask
):
    req_rows, feat_share = query_flat.shape
    pool_pages, page_len = (key_pool.shape[0], key_pool.shape[1])
    slot_count = local_table.shape[1]
    page_ids = jnp.arange(pool_pages, dtype=jnp.int32)
    slot_ids = jnp.arange(slot_count, dtype=jnp.int32)
    slot_used = slot_ids[None, :] * page_len < lengths[:, None]
    page_hit = (local_table[:, :, None] == page_ids[None, None, :]) & slot_used[:, :, None]
    start_pos = jnp.sum(jnp.where(page_hit, slot_ids[None, :, None] * page_len, 0), axis=1)
    is_owned = jnp.any(page_hit, axis=1)
    position = start_pos[:, :, None] + jnp.arange(page_len, dtype=jnp.int32)[None, None, :]
    is_valid = (is_owned[:, :, None] & (position < lengths[:, None, None])).reshape(
        req_rows, pool_pages * page_len
    )
    flat_keys = key_pool.reshape(pool_pages * page_len, feat_share)
    flat_values = value_pool.reshape(pool_pages * page_len, feat_share)
    query_wide = spread_query(query_flat, mask)
    scores = (
        jnp.einsum("rhf,tf->rht", query_wide, flat_keys, preferred_element_type=jnp.float32)
        * score_scale
    )
    scores = jnp.where(is_valid[:, None, :], scores, -jnp.inf)
    own_score = own_scores(query_flat, key_new, mask, score_scale)

    def mix_pool(cache_weights):
        return jnp.einsum(
            "rht,tf->rhf", cache_weights, flat_values, preferred_element_type=jnp.float32
        )

    return finish_mix(scores, own_score, value_new, mask, mix_pool)


def local(
    tokens,
    deal_order,
    page_table,
    lengths,
    qkv_weight,
    out_weight,
    up_weight,
    down_weight,
    key_cache,
    value_cache,
    attn_norm,
    mlp_norm,
):
    req_rows, model_width = tokens.shape
    tp_count = lax.axis_size("tp")
    req_index = lax.axis_index("req")
    feat_share = model_width // tp_count
    score_scale = 1.0 / math.sqrt(HD)
    mask = head_masks(feat_share, HD)
    dealt_here = lax.dynamic_slice_in_dim(deal_order, req_index * req_rows, req_rows)
    everyone = lax.all_gather(tokens, "req", axis=0, tiled=True)
    current = jnp.take(everyone, dealt_here, axis=0)
    pool_pages = key_cache.shape[1]
    local_table = page_table - req_index * pool_pages
    qkv_flat = qkv_weight.reshape(model_width, 3 * feat_share)
    for layer_index in range(key_cache.shape[0]):
        projected = jnp.dot(current, qkv_flat, preferred_element_type=jnp.float32).astype(
            jnp.bfloat16
        )
        query_flat = projected[:, :feat_share]
        key_new = projected[:, feat_share : 2 * feat_share]
        value_new = projected[:, 2 * feat_share :]
        key_pool = key_cache[layer_index]
        value_pool = value_cache[layer_index]
        attended = attend_pool(
            query_flat,
            key_new,
            value_new,
            key_pool,
            value_pool,
            local_table,
            lengths,
            score_scale,
            mask,
        )
        attended = attended.astype(jnp.bfloat16)
        attn_term = jnp.dot(attended, out_weight, preferred_element_type=jnp.float32)
        hidden = post_norm(attn_term, current, attn_norm)
        up_proj = jnp.dot(hidden, up_weight, preferred_element_type=jnp.float32)
        activated = jax.nn.gelu(up_proj, approximate=True).astype(jnp.bfloat16)
        down_term = jnp.dot(activated, down_weight, preferred_element_type=jnp.float32)
        current = post_norm(down_term, hidden, mlp_norm)
    request_count = deal_order.shape[0]
    inverse = (
        jnp.zeros_like(deal_order).at[deal_order].set(jnp.arange(request_count, dtype=jnp.int32))
    )
    inverse_here = lax.dynamic_slice_in_dim(inverse, req_index * req_rows, req_rows)
    returned = lax.all_gather(current, "req", axis=0, tiled=True)
    result = jnp.take(returned, inverse_here, axis=0)
    return result


def solution(mesh):
    in_specs = (
        P("req", None),
        P(),
        P("req", None),
        P("req"),
        P(None, None, "tp"),
        P("tp", None),
        P(None, "tp"),
        P("tp", None),
        P(None, "req", None, "tp"),
        P(None, "req", None, "tp"),
        P(),
        P(),
    )
    out_specs = P("req", None)
    return jax.shard_map(local, mesh=mesh, in_specs=in_specs, out_specs=out_specs, check_vma=False)
```

profile of v0, /device:TPU:1, one launch (start us, length us, event | category | flops | bytes accessed | tf_op | source)
XLA Modules:
  0.0 334.8 jit_solution(1223456797249646341)
XLA Ops:
  6.5 0.7 all-gather.3.cloned.1.call-update
  7.3 8.8 %copy.16 = bf16[2048,3,512]{0,2,1:T(8,128)(2,1)} copy(bf16[2048,3,512]{2,0,1:T(8,128)(2,1)} %param.18) | data formatting | bytes 12582912 | tf_op args[4]
  16.4 0.1 fusion.41
  16.5 0.1 select_reduce_fusion.4
  16.7 9.8 %fusion.77 = (bf16[1,42,128,512]{3,2,1,0:T(8,128)(2,1)}, bf16[1,42,128,512]{3,2,1,0:T(8,128)(2,1)}) fusion(bf16[2,42,128,512]{3,2,1,0:T(8,128)(2,1)} %param.22), kind=kLoop, calls=%fused_computation.147 | loop fusion | bytes 22020096 | tf_op jit(solution)/shard_map/slice | solution.py:122
  26.4 9.7 %fusion.78 = (bf16[1,42,128,512]{3,2,1,0:T(8,128)(2,1)}, bf16[1,42,128,512]{3,2,1,0:T(8,128)(2,1)}) fusion(bf16[2,42,128,512]{3,2,1,0:T(8,128)(2,1)} %param.23), kind=kLoop, calls=%fused_computation.148 | loop fusion | bytes 22020096 | tf_op jit(solution)/shard_map/slice | solution.py:123
  36.2 0.3 add.173
  36.4 0.3 and.65
  36.7 0.3 fusion.11
  37.0 22.6 %all-gather.3.cloned.1.call-done = bf16[1024,2048]{1,0:T(8,128)(2,1)} async-done(((bf16[32,2048]{1,0:T(8,128)(2,1)}), bf16[1024,2048]{1,0:T(8,128)(2,1)}) %all-gather.3.cloned.1.call-update) | async-done | bytes 4194320 | tf_op jit(solution)/shard_map/all_gather | solution.py:110
  59.7 3.5 %gather_fusion = bf16[32,2048]{1,0:T(8,128)(2,1)S(1)} fusion(bf16[1024,2048]{1,0:T(8,128)(2,1)} %all-gather.3.cloned.1.call-done, s32[1024]{0:T(1024)S(1)} %pad_clamp_fusion.1), kind=kCustom, calls=%fused_computation.clone | custom fusion | bytes 262272 | tf_op jit(solution)/shard_map/jit(_take)/gather | solution.py:111
  63.2 4.9 %convolution_convert_fusion.1 = bf16[32,1536]{1,0:T(8,128)(2,1)S(1)} fusion(bf16[2048,1536]{0,1:T(8,128)(2,1)} %bitcast.44, bf16[32,2048]{1,0:T(8,128)(2,1)S(1)} %gather_fusion, pred[32]{0:T(512)(128)(4,1)S(1)} %get-tuple-element.8), kind=kOutput, calls=%fused_computation.14 | convolution fusion | flops 201441280 | bytes 6520864 | tf_op jit(solution)/shard_map/dot_general | solution.py:116
  68.2 0.1 select_reduce_fusion.3
  68.3 2.0 fusion.81
  70.3 0.5 fusion.2
  70.9 0.1 select_reduce_fusion.2
  71.0 1.0 fusion.8
  72.1 1.1 convolution_convert_fusion.5
  73.3 38.0 %all-reduce.5.cloned.1.call-done = bf16[32,2048]{1,0:T(8,128)(2,1)} async-done(((bf16[32,2048]{1,0:T(8,128)(2,1)}), bf16[32,2048]{1,0:T(8,128)(2,1)}) %all-reduce.5.cloned.1.call-update) | async-done | bytes 131088 | tf_op jit(solution)/shard_map/psum | solution.py:21
  111.3 1.1 fusion.13
  112.5 1.1 multiply_reduce_fusion.3
  113.6 1.1 add_convert_fusion.3
  114.7 5.7 %convolution_convert_fusion.4 = bf16[32,2048]{1,0:T(8,128)(2,1)} fusion(bf16[1024,2048]{1,0:T(8,128)(2,1)} %param.21, bf16[32,2048]{1,0:T(8,128)(2,1)S(1)} %add_convert_fusion.3, bf16[2048,1024]{1,0:T(8,128)(2,1)} %param.20), kind=kOutput, calls=%fused_computation.17 | convolution fusion | flops 268795904 | bytes 8650752 | tf_op jit(solution)/shard_map/dot_general | solution.py:140
  120.5 0.2 all-reduce.9.cloned.1.call-start
  120.7 41.5 %all-reduce.7.cloned.1.call-done = bf16[32,2048]{1,0:T(8,128)(2,1)} async-done(((bf16[32,2048]{1,0:T(8,128)(2,1)}), bf16[32,2048]{1,0:T(8,128)(2,1)}) %all-reduce.7.cloned.1.call-update) | async-done | bytes 131088 | tf_op jit(solution)/shard_map/psum | solution.py:21
  162.2 1.0 fusion.15
  163.3 1.1 multiply_reduce_fusion.2
  164.4 1.0 add_convert_fusion.2
  165.4 4.9 %convolution_convert_fusion = bf16[32,1536]{1,0:T(8,128)(2,1)S(1)} fusion(bf16[32,2048]{1,0:T(8,128)(2,1)S(1)} %add_convert_fusion.2, bf16[2048,1536]{0,1:T(8,128)(2,1)} %bitcast.45), kind=kOutput, calls=%fused_computation.13 | convolution fusion | flops 201375744 | bytes 6520832 | tf_op jit(solution)/shard_map/dot_general | solution.py:116
  170.3 0.1 select_reduce_fusion.1
  170.5 4.7 %fusion.82 = (f32[32,4]{0,1:T(4,128)S(1)}, f32[32,4,5376]{2,0,1:T(8,128)S(1)}) fusion(bf16[5376,512,1]{1,0,2:T(8,128)(2,1)} %bitcast.46, pred[4,512]{1,0:T(4,128)(4,1)S(1)} %iota_compare_fusion.1, bf16[32,512]{1,0:T(8,128)(2,1)S(1)} %slice.67, pred[32,5376]{1,0:T(8,128)(4,1)S(1)} %fusion.11), kind=kOutput, calls=%fused_computation.152 | convolution fusion | flops 706772864 | bytes 8464896 | tf_op jit(solution)/shard_map/rhf,tf->rht/dot_general | solution.py:75
  175.1 0.5 fusion.3
  175.7 0.1 select_reduce_fusion
  175.8 1.0 fusion.9
  176.9 1.1 convolution_convert_fusion.3
  178.1 41.7 %all-reduce.9.cloned.1.call-done = bf16[32,2048]{1,0:T(8,128)(2,1)} async-done(((bf16[32,2048]{1,0:T(8,128)(2,1)}), bf16[32,2048]{1,0:T(8,128)(2,1)}) %all-reduce.9.cloned.1.call-update) | async-done | bytes 131088 | tf_op jit(solution)/shard_map/psum | solution.py:21
  219.7 1.0 fusion.17
  220.8 1.1 multiply_reduce_fusion.1
  221.9 1.0 add_convert_fusion.1
  222.9 5.7 %convolution_convert_fusion.2 = bf16[32,2048]{1,0:T(8,128)(2,1)} fusion(bf16[1024,2048]{1,0:T(8,128)(2,1)} %param.21, bf16[32,2048]{1,0:T(8,128)(2,1)S(1)} %add_convert_fusion.1, bf16[2048,1024]{1,0:T(8,128)(2,1)} %param.20), kind=kOutput, calls=%fused_computation.15 | convolution fusion | flops 268795904 | bytes 8650752 | tf_op jit(solution)/shard_map/dot_general | solution.py:140
  228.7 41.7 %all-reduce.11.cloned.1.call-done = bf16[32,2048]{1,0:T(8,128)(2,1)} async-done(((bf16[32,2048]{1,0:T(8,128)(2,1)}), bf16[32,2048]{1,0:T(8,128)(2,1)}) %all-reduce.11.cloned.1.call-update) | async-done | bytes 131088 | tf_op jit(solution)/shard_map/psum | solution.py:21
  270.4 1.0 fusion.19
  271.5 1.1 multiply_reduce_fusion
  272.6 1.7 add_convert_fusion
  274.3 4.3 %scatter_custom_fusion = s32[1024]{0:T(1024)S(1)} fusion(s32[1024]{0:T(1024)S(1)} %compare_select_fusion, s32[1024]{0:T(1024)S(1)} %iota.51, s32[]{:T(128)} %constant.32.clone.1), kind=kCustom, calls=%fused_computation.111 | custom fusion | bytes 4100 | tf_op jit(solution)/shard_map/scatter | solution.py:144
  278.7 45.0 %all-gather.5.cloned.1.call-done = bf16[1024,2048]{1,0:T(8,128)(2,1)} async-done(((bf16[32,2048]{1,0:T(8,128)(2,1)}), bf16[1024,2048]{1,0:T(8,128)(2,1)}) %all-gather.5.cloned.1.call-update) | async-done | bytes 4194320 | tf_op jit(solution)/shard_map/all_gather | solution.py:147
  323.7 3.5 %gather_fusion.1 = bf16[32,2048]{1,0:T(8,128)(2,1)S(1)} fusion(bf16[1024,2048]{1,0:T(8,128)(2,1)} %all-gather.5.cloned.1.call-done, s32[1024]{0:T(1024)S(1)} %pad_clamp_fusion), kind=kCustom, calls=%fused_computation.1.clone | custom fusion | bytes 262272 | tf_op jit(solution)/shard_map/jit(_take)/gather | solution.py:148
  327.2 0.7 broadcast_select_fusion
  (64 shorter events, 0.8 us)
Async XLA Ops:
  6.5 65.5 %copy-start = (bf16[512,2048]{1,0:T(8,128)(2,1)S(1)}, bf16[512,2048]{1,0:T(8,128)(2,1)}, u32[]{:S(2)}) copy-start(bf16[512,2048]{1,0:T(8,128)(2,1)} %param.19) | copy-start | bytes 6291460
  6.5 53.1 %all-gather.3.cloned.1.call-start = ((), (), s32[]{:S(2)}) async-start(), calls=%async_computation | async-start | bytes 4325376 | tf_op jit(solution)/shard_map/all_gather | solution.py:110
  7.3 104.1 %all-reduce.5.cloned.1.call-start = ((), (), s32[]{:S(2)}) async-start(), calls=%async_computation.1 | async-start | bytes 262144 | tf_op jit(solution)/shard_map/psum | solution.py:21
  7.3 8.9 %copy-start.4 = (s32[1024]{0:T(1024)S(1)}, s32[1024]{0:T(1024)}, u32[]{:S(2)}) copy-start(s32[1024]{0:T(1024)} %param.15) | copy-start | bytes 12292
  7.3 9.0 %copy-start.6 = (s32[32]{0:T(128)S(1)}, s32[32]{0:T(128)}, u32[]{:S(2)}) copy-start(s32[32]{0:T(128)} %param.17) | copy-start | bytes 388
  7.3 9.1 %copy-start.5 = (s32[32,6]{0,1:T(8,128)S(1)}, s32[32,6]{0,1:T(8,128)}, u32[]{:S(2)}) copy-start(s32[32,6]{0,1:T(8,128)} %param.16) | copy-start | bytes 2308
  63.2 5.1 %copy-start.1 = (bf16[1,42,128,512]{3,2,1,0:T(8,128)(2,1)S(1)}, bf16[1,42,128,512]{3,2,1,0:T(8,128)(2,1)}, u32[]{:S(2)}) copy-start(bf16[1,42,128,512]{3,2,1,0:T(8,128)(2,1)} %get-tuple-element.11) | copy-start | bytes 16515076
  68.1 2.9 slice-start.2
  68.3 2.7 slice-start.3
  71.0 2.3 copy-start.2
  73.2 89.0 %all-reduce.7.cloned.1.call-start = ((), (), s32[]{:S(2)}) async-start(), calls=%async_computation.2 | async-start | bytes 262144 | tf_op jit(solution)/shard_map/psum | solution.py:21
  114.7 6.0 %copy-start.3 = (f32[2,2048]{1,0:T(2,128)S(1)}, f32[2,2048]{1,0:T(2,128)}, u32[]{:S(2)}) copy-start(f32[2,2048]{1,0:T(2,128)} %param.25) | copy-start | bytes 49156
  120.5 99.3 %all-reduce.9.cloned.1.call-start = ((), (), s32[]{:S(2)}) async-start(), calls=%async_computation.3 | async-start | bytes 262144 | tf_op jit(solution)/shard_map/psum | solution.py:21
  165.4 10.4 %slice-start = ((s8[5505024]{0:T(1024)(128)(4,1)}), s8[4194304]{0:T(1024)(128)(4,1)S(1)}, s32[]{:S(2)}) async-start(s8[5505024]{0:T(1024)(128)(4,1)} %bitcast.48), calls=%async_computation.6 | async-start | bytes 8388608
  170.5 5.4 %slice-start.1 = ((s8[5505024]{0:T(1024)(128)(4,1)}), s8[1310720]{0:T(1024)(128)(4,1)S(1)}, s32[]{:S(2)}) async-start(s8[5505024]{0:T(1024)(128)(4,1)} %bitcast.48), calls=%async_computation.7 | async-start | bytes 2621440
  178.0 92.4 %all-reduce.11.cloned.1.call-start = ((), (), s32[]{:S(2)}) async-start(), calls=%async_computation.4 | async-start | bytes 262144 | tf_op jit(solution)/shard_map/psum | solution.py:21
  228.7 95.1 %all-gather.5.cloned.1.call-start = ((), (), s32[]{:S(2)}) async-start(), calls=%async_computation.5 | async-start | bytes 4325376 | tf_op jit(solution)/shard_map/all_gather | solution.py:147
Sparse Core Ops, SparseCore 0:
  9.6 50.0 all-gather.2
  73.3 37.9 all-reduce.4
  120.6 41.5 all-reduce.6
  178.1 41.5 all-reduce.8
  228.8 41.5 all-reduce.10
  274.4 49.2 all-gather.4
where the time goes:
time: 335 us
  waiting for transfers between devices  231 us (69%)
  local copies, waits for them, and re-layouts  40.3 us (12%)
  matrix products  32.2 us (10%)
  other arithmetic  16.7 us (5%)
  between operations  13.9 us (4%)
    psum x4, waiting for transfers between devices, post_norm(): lax.psum(partial_term.astype(jnp.bfloat16), 'tp').astype(jnp.float32)  163 us
    all_gather x1, waiting for transfers between devices, local(): returned = lax.all_gather(current, 'req', axis=0, tiled=True)  45 us
    all_gather x1, waiting for transfers between devices, local(): everyone = lax.all_gather(tokens, 'req', axis=0, tiled=True)  22.6 us
    dot_general x2, matrix products, local(): jnp.dot(activated, down_weight, preferred_element_type=jnp.float32)  11.4 us
    dot_general x2, matrix products, local(): jnp.dot(current, qkv_flat, preferred_element_type=jnp.float32)  9.8 us
    slice x1, local copies, waits for them, and re-layouts, local(): key_pool = key_cache[layer_index]  9.76 us
    slice x1, local copies, waits for them, and re-layouts, local(): value_pool = value_cache[layer_index]  9.75 us
    unnamed x23, local copies, waits for them, and re-layouts  8.92 us
  transfers between devices with their start and end apart: 6, of which 6 were waited for; matrix products, arithmetic and copies ran while one was open for 10% of the time, Pallas kernels for 0%

commit v1 on v0

--- a/solution.py
+++ b/solution.py
@@ -18,7 +18,7 @@
 
 
 def post_norm(partial_term, residual, gain_bias):
-    row_total = lax.psum(partial_term.astype(jnp.bfloat16), "tp").astype(
+    row_total = jnp.sum(lax.all_gather(partial_term.astype(jnp.bfloat16), "tp"), axis=0).astype(
         jnp.float32
     ) + residual.astype(jnp.float32)
     return layer_norm(row_total, gain_bias)

time: 335 us -> 207 us (0.62)
  waiting for transfers between devices: 231 us -> 75.4 us
  blocking collectives: 0 us -> 40.9 us
  other arithmetic: 16.7 us -> 6.21 us
    psum x4 -> x0, waiting for transfers between devices: 163 us -> none  [post_norm(): lax.psum(partial_term.astype(jnp.bfloat16), 'tp').astype(jnp.float32)]
    all_gather x0 -> x4, blocking collectives: none -> 40.9 us  [post_norm(): lax.all_gather(partial_term.astype(jnp.bfloat16), 'tp')]
    all_gather x1, waiting for transfers between devices: 45 us -> 52.2 us  [local(): returned = lax.all_gather(current, 'req', axis=0, tiled=True)]
    reduce_sum x4, other arithmetic: 4.49 us -> 0.87 us  [layer_norm(): row_var = jnp.mean(centered * centered, axis=-1, keepdims=True)]
    convert_element_type x4, other arithmetic: 4.8 us -> 1.18 us  [layer_norm(): (centered * lax.rsqrt(row_var + epsilon) * gain_bias[0] + gain_bias[1]).a...]
    reduce_sum x4, other arithmetic: 4.26 us -> 0.67 us  [layer_norm(): row_mean = jnp.mean(row_total, axis=-1, keepdims=True)]
  transfers between devices with their start and end apart: 6 -> 2, of which waited for: 6 -> 2; matrix products, arithmetic and copies ran while one was open for 10% -> 17% of each run, Pallas kernels for 0% -> 0%
where the time goes in v1:
time: 207 us; the launch traced here: 206 us
  waiting for transfers between devices  75.4 us (36%)
  blocking collectives  40.9 us (20%)
  local copies, waits for them, and re-layouts  40.3 us (19%)
  matrix products  29.5 us (14%)
  between operations  13.8 us (7%)
  other arithmetic  6.21 us (3%)
    all_gather x1, waiting for transfers between devices, local(): returned = lax.all_gather(current, 'req', axis=0, tiled=True)  52.2 us
    all_gather x4, blocking collectives, post_norm(): lax.all_gather(partial_term.astype(jnp.bfloat16), 'tp')  40.9 us
    all_gather x1, waiting for transfers between devices, local(): everyone = lax.all_gather(tokens, 'req', axis=0, tiled=True)  22.6 us
    dot_general x2, matrix products, local(): jnp.dot(activated, down_weight, preferred_element_type=jnp.float32)  10.1 us
    dot_general x2, matrix products, local(): jnp.dot(current, qkv_flat, preferred_element_type=jnp.float32)  9.8 us
    slice x1, local copies, waits for them, and re-layouts, local(): key_pool = key_cache[layer_index]  9.75 us
    slice x1, local copies, waits for them, and re-layouts, local(): value_pool = value_cache[layer_index]  9.75 us
    unnamed x23, local copies, waits for them, and re-layouts  8.92 us
  transfers between devices with their start and end apart: 2, of which 2 were waited for; matrix products, arithmetic and copies ran while one was open for 17% of the time, Pallas kernels for 0%

profile of v1, /device:TPU:1, one launch (start us, length us, event | category | flops | bytes accessed | tf_op | source)
XLA Modules:
  0.0 206.2 jit_solution(6817273022081315544)
XLA Ops:
  6.5 0.7 all-gather.7.cloned.1.call-update
  7.4 8.9 %copy.16 = bf16[2048,3,512]{0,2,1:T(8,128)(2,1)} copy(bf16[2048,3,512]{2,0,1:T(8,128)(2,1)} %param.18) | data formatting | bytes 12582912 | tf_op args[4]
  16.4 0.1 fusion.41
  16.5 0.1 select_reduce_fusion.4
  16.8 9.8 %fusion.77 = (bf16[1,42,128,512]{3,2,1,0:T(8,128)(2,1)}, bf16[1,42,128,512]{3,2,1,0:T(8,128)(2,1)}) fusion(bf16[2,42,128,512]{3,2,1,0:T(8,128)(2,1)} %param.22), kind=kLoop, calls=%fused_computation.147 | loop fusion | bytes 22020096 | tf_op jit(solution)/shard_map/slice | solution.py:122
  26.5 9.7 %fusion.78 = (bf16[1,42,128,512]{3,2,1,0:T(8,128)(2,1)}, bf16[1,42,128,512]{3,2,1,0:T(8,128)(2,1)}) fusion(bf16[2,42,128,512]{3,2,1,0:T(8,128)(2,1)} %param.23), kind=kLoop, calls=%fused_computation.148 | loop fusion | bytes 22020096 | tf_op jit(solution)/shard_map/slice | solution.py:123
  36.3 0.3 add.165
  36.5 0.3 and.65
  36.8 0.3 fusion.11
  37.1 22.6 %all-gather.7.cloned.1.call-done = bf16[1024,2048]{1,0:T(8,128)(2,1)} async-done(((bf16[32,2048]{1,0:T(8,128)(2,1)}), bf16[1024,2048]{1,0:T(8,128)(2,1)}) %all-gather.7.cloned.1.call-update) | async-done | bytes 4194320 | tf_op jit(solution)/shard_map/all_gather | solution.py:110
  59.7 3.5 %gather_fusion = bf16[32,2048]{1,0:T(8,128)(2,1)S(1)} fusion(bf16[1024,2048]{1,0:T(8,128)(2,1)} %all-gather.7.cloned.1.call-done, s32[1024]{0:T(1024)S(1)} %pad_clamp_fusion.1), kind=kCustom, calls=%fused_computation.clone | custom fusion | bytes 262272 | tf_op jit(solution)/shard_map/jit(_take)/gather | solution.py:111
  63.2 4.9 %convolution_convert_fusion.1 = bf16[32,1536]{1,0:T(8,128)(2,1)S(1)} fusion(bf16[2048,1536]{0,1:T(8,128)(2,1)} %bitcast.48, bf16[32,2048]{1,0:T(8,128)(2,1)S(1)} %gather_fusion, pred[32]{0:T(512)(128)(4,1)S(1)} %get-tuple-element.8), kind=kOutput, calls=%fused_computation.14 | convolution fusion | flops 201441280 | bytes 6520864 | tf_op jit(solution)/shard_map/dot_general | solution.py:116
  68.2 0.1 select_reduce_fusion.3
  68.3 2.0 fusion.81
  70.3 0.5 fusion.2
  70.9 0.1 select_reduce_fusion.2
  71.0 1.0 fusion.8
  72.1 0.5 convolution_convert_fusion.5
  72.5 11.0 %all-gather = bf16[128,2048]{1,0:T(8,128)(2,1)S(1)} all-gather(bf16[32,2048]{1,0:T(8,128)(2,1)S(1)} %convolution_convert_fusion.5), channel_id=2, replica_groups=mesh['req'=32,'tp'=4] {'tp'}, dimensions={0}, use_global_device_ids=true | all-gather | bytes 655360 | tf_op jit(solution)/shard_map/all_gather | solution.py:21
  83.6 0.2 fusion.13
  83.9 0.2 multiply_reduce_fusion.3
  84.1 0.2 add_convert_fusion.3
  84.3 5.0 %convolution_convert_fusion.4 = bf16[32,2048]{1,0:T(8,128)(2,1)S(1)} fusion(bf16[1024,2048]{1,0:T(8,128)(2,1)} %param.21, bf16[32,2048]{1,0:T(8,128)(2,1)S(1)} %add_convert_fusion.3, bf16[2048,1024]{1,0:T(8,128)(2,1)} %param.20), kind=kOutput, calls=%fused_computation.17 | convolution fusion | flops 268795904 | bytes 8650752 | tf_op jit(solution)/shard_map/dot_general | solution.py:140
  89.3 10.1 %all-gather.1 = bf16[128,2048]{1,0:T(8,128)(2,1)S(1)} all-gather(bf16[32,2048]{1,0:T(8,128)(2,1)S(1)} %convolution_convert_fusion.4), channel_id=3, replica_groups=mesh['req'=32,'tp'=4] {'tp'}, dimensions={0}, use_global_device_ids=true | all-gather | bytes 655360 | tf_op jit(solution)/shard_map/all_gather | solution.py:21
  99.5 0.1 fusion.15
  99.6 0.2 multiply_reduce_fusion.2
  99.9 0.1 add_convert_fusion.2
  100.0 4.9 %convolution_convert_fusion = bf16[32,1536]{1,0:T(8,128)(2,1)S(1)} fusion(bf16[32,2048]{1,0:T(8,128)(2,1)S(1)} %add_convert_fusion.2, bf16[2048,1536]{0,1:T(8,128)(2,1)} %bitcast.49), kind=kOutput, calls=%fused_computation.13 | convolution fusion | flops 201375744 | bytes 6520832 | tf_op jit(solution)/shard_map/dot_general | solution.py:116
  104.9 0.1 select_reduce_fusion.1
  105.1 4.7 %fusion.82 = (f32[32,4]{0,1:T(4,128)S(1)}, f32[32,4,5376]{2,0,1:T(8,128)S(1)}) fusion(bf16[5376,512,1]{1,0,2:T(8,128)(2,1)} %bitcast.50, pred[4,512]{1,0:T(4,128)(4,1)S(1)} %iota_compare_fusion.1, bf16[32,512]{1,0:T(8,128)(2,1)S(1)} %slice.67, pred[32,5376]{1,0:T(8,128)(4,1)S(1)} %fusion.11), kind=kOutput, calls=%fused_computation.152 | convolution fusion | flops 706772864 | bytes 8464896 | tf_op jit(solution)/shard_map/rhf,tf->rht/dot_general | solution.py:75
  109.7 0.5 fusion.3
  110.3 0.1 select_reduce_fusion
  110.4 1.0 fusion.9
  111.4 0.5 convolution_convert_fusion.3
  111.9 9.9 %all-gather.2 = bf16[128,2048]{1,0:T(8,128)(2,1)S(1)} all-gather(bf16[32,2048]{1,0:T(8,128)(2,1)S(1)} %convolution_convert_fusion.3), channel_id=4, replica_groups=mesh['req'=32,'tp'=4] {'tp'}, dimensions={0}, use_global_device_ids=true | all-gather | bytes 655360 | tf_op jit(solution)/shard_map/all_gather | solution.py:21
  121.9 0.1 fusion.17
  122.0 0.2 multiply_reduce_fusion.1
  122.3 0.1 add_convert_fusion.1
  122.4 5.0 %convolution_convert_fusion.2 = bf16[32,2048]{1,0:T(8,128)(2,1)S(1)} fusion(bf16[1024,2048]{1,0:T(8,128)(2,1)} %param.21, bf16[32,2048]{1,0:T(8,128)(2,1)S(1)} %add_convert_fusion.1, bf16[2048,1024]{1,0:T(8,128)(2,1)} %param.20), kind=kOutput, calls=%fused_computation.15 | convolution fusion | flops 268795904 | bytes 8650752 | tf_op jit(solution)/shard_map/dot_general | solution.py:140
  127.4 9.9 %all-gather.3 = bf16[128,2048]{1,0:T(8,128)(2,1)S(1)} all-gather(bf16[32,2048]{1,0:T(8,128)(2,1)S(1)} %convolution_convert_fusion.2), channel_id=5, replica_groups=mesh['req'=32,'tp'=4] {'tp'}, dimensions={0}, use_global_device_ids=true | all-gather | bytes 655360 | tf_op jit(solution)/shard_map/all_gather | solution.py:21
  137.4 0.1 fusion.19
  137.6 0.2 multiply_reduce_fusion
  137.8 0.8 add_convert_fusion
  138.6 4.3 %scatter_custom_fusion = s32[1024]{0:T(1024)S(1)} fusion(s32[1024]{0:T(1024)S(1)} %compare_select_fusion, s32[1024]{0:T(1024)S(1)} %iota.51, s32[]{:T(128)} %constant.32.clone.1), kind=kCustom, calls=%fused_computation.111 | custom fusion | bytes 4100 | tf_op jit(solution)/shard_map/scatter | solution.py:144
  142.9 0.1 compare_and_fusion
  143.0 52.2 %all-gather.9.cloned.1.call-done = bf16[1024,2048]{1,0:T(8,128)(2,1)} async-done(((bf16[32,2048]{1,0:T(8,128)(2,1)}), bf16[1024,2048]{1,0:T(8,128)(2,1)}) %all-gather.9.cloned.1.call-update) | async-done | bytes 4194320 | tf_op jit(solution)/shard_map/all_gather | solution.py:147
  195.2 3.5 %gather_fusion.1 = bf16[32,2048]{1,0:T(8,128)(2,1)S(1)} fusion(bf16[1024,2048]{1,0:T(8,128)(2,1)} %all-gather.9.cloned.1.call-done, s32[1024]{0:T(1024)S(1)} %pad_clamp_fusion), kind=kCustom, calls=%fused_computation.1.clone | custom fusion | bytes 262272 | tf_op jit(solution)/shard_map/jit(_take)/gather | solution.py:148
  198.7 0.7 broadcast_select_fusion
  (60 shorter events, 0.8 us)
Async XLA Ops:
  6.5 65.5 %copy-start = (bf16[512,2048]{1,0:T(8,128)(2,1)S(1)}, bf16[512,2048]{1,0:T(8,128)(2,1)}, u32[]{:S(2)}) copy-start(bf16[512,2048]{1,0:T(8,128)(2,1)} %param.19) | copy-start | bytes 6291460
  6.5 53.1 %all-gather.7.cloned.1.call-start = ((), (), s32[]{:S(2)}) async-start(), calls=%async_computation | async-start | bytes 4325376 | tf_op jit(solution)/shard_map/all_gather | solution.py:110
  7.3 187.9 %all-gather.9.cloned.1.call-start = ((), (), s32[]{:S(2)}) async-start(), calls=%async_computation.1 | async-start | bytes 4325376 | tf_op jit(solution)/shard_map/all_gather | solution.py:147
  7.3 8.9 %copy-start.4 = (s32[1024]{0:T(1024)S(1)}, s32[1024]{0:T(1024)}, u32[]{:S(2)}) copy-start(s32[1024]{0:T(1024)} %param.15) | copy-start | bytes 12292
  7.3 9.0 %copy-start.6 = (s32[32]{0:T(128)S(1)}, s32[32]{0:T(128)}, u32[]{:S(2)}) copy-start(s32[32]{0:T(128)} %param.17) | copy-start | bytes 388
  7.3 9.1 %copy-start.5 = (s32[32,6]{0,1:T(8,128)S(1)}, s32[32,6]{0,1:T(8,128)}, u32[]{:S(2)}) copy-start(s32[32,6]{0,1:T(8,128)} %param.16) | copy-start | bytes 2308
  7.3 9.4 %copy-start.2 = (f32[2,2048]{1,0:T(2,128)S(1)}, f32[2,2048]{1,0:T(2,128)}, u32[]{:S(2)}) copy-start(f32[2,2048]{1,0:T(2,128)} %param.24) | copy-start | bytes 49156
  7.4 9.4 %copy-start.3 = (f32[2,2048]{1,0:T(2,128)S(1)}, f32[2,2048]{1,0:T(2,128)}, u32[]{:S(2)}) copy-start(f32[2,2048]{1,0:T(2,128)} %param.25) | copy-start | bytes 49156
  63.2 5.1 %copy-start.1 = (bf16[1,42,128,512]{3,2,1,0:T(8,128)(2,1)S(1)}, bf16[1,42,128,512]{3,2,1,0:T(8,128)(2,1)}, u32[]{:S(2)}) copy-start(bf16[1,42,128,512]{3,2,1,0:T(8,128)(2,1)} %get-tuple-element.11) | copy-start | bytes 16515076
  68.1 2.9 %slice-start.2 = ((s8[5505024]{0:T(1024)(128)(4,1)}), s8[4194304]{0:T(1024)(128)(4,1)S(1)}, s32[]{:S(2)}) async-start(s8[5505024]{0:T(1024)(128)(4,1)} %bitcast.55), calls=%async_computation.4 | async-start | bytes 8388608
  68.3 2.7 %slice-start.3 = ((s8[5505024]{0:T(1024)(128)(4,1)}), s8[1310720]{0:T(1024)(128)(4,1)S(1)}, s32[]{:S(2)}) async-start(s8[5505024]{0:T(1024)(128)(4,1)} %bitcast.55), calls=%async_computation.5 | async-start | bytes 2621440
  100.0 10.4 %slice-start = ((s8[5505024]{0:T(1024)(128)(4,1)}), s8[4194304]{0:T(1024)(128)(4,1)S(1)}, s32[]{:S(2)}) async-start(s8[5505024]{0:T(1024)(128)(4,1)} %bitcast.52), calls=%async_computation.2 | async-start | bytes 8388608
  105.0 5.4 %slice-start.1 = ((s8[5505024]{0:T(1024)(128)(4,1)}), s8[1310720]{0:T(1024)(128)(4,1)S(1)}, s32[]{:S(2)}) async-start(s8[5505024]{0:T(1024)(128)(4,1)} %bitcast.52), calls=%async_computation.3 | async-start | bytes 2621440
Sparse Core Ops, SparseCore 0:
  9.6 50.0 all-gather.6
  138.7 56.4 all-gather.8
